TPU v7x, 32 devices: a whole 2x2x4 slice. The times are simulated.
32 devices in a mesh: grp: 2 (over y), tgt: 4 (over z), shot: 4 (over x, core).
Axes of the slice: x: 2, y: 2, z: 4, core: 2. Of those that a mesh axis runs over, the one named last changes fastest.
Arguments:
- adjoint_now: float32 [8, 16, 32, 256], P(('grp', 'shot'), 'tgt'), parts along dimension 0, may hold values from -6 to 6
- adjoint_later: float32 [8, 16, 32, 256], P(('grp', 'shot'), 'tgt'), parts along dimension 0, may hold values from -6 to 6
- courant: float32 [16, 32, 256], P('tgt'), may hold values from 0.15 to 0.45
- fwd_acc: bfloat16 [8, 4, 16, 32, 256], P(('grp', 'shot'), None, 'tgt'), parts along dimension 0, may hold values from -6 to 6
- surf_dest: int32 [1024, 1], P('tgt'), may hold values from 0 to 3; in each aligned block of 256 rows (0 to 255, 256 to 511, ...) at most 128 rows name the same one
- surf_cell: int32 [1024], P('tgt'), may hold values from 0 to 32767
- surf_vals: float32 [8, 4, 1024], P(('grp', 'shot'), None, 'tgt'), parts along dimension 0, may hold values from -6 to 6
Outputs:
- adjoint_final: float32 [8, 16, 32, 256], P(('grp', 'shot'), 'tgt'), parts along dimension 0
- grad: float32 [32, 32, 256], P(('grp', 'tgt')), parts along dimension 0
There are 2 independent parts, one for each index of `grp`. A program takes and returns all parts, laid end to end along the dimension named above; an argument that names none is the same for every part. Nothing has to cross between parts.
Inputs may be any that keep to these rules, and one draw needn't show every extreme that they name: `surf_dest`: in each owner's list of 256 entries at most 128 entries name one slab, a bound that some block reaches of them; every slab is named somewhere. `surf_cell`: several entries may name the same cell; their values add.
All inputs are finite; a program needn't handle non-finite values.
Results may differ from a plain program's by a relative error of at most 0.0003.
Values sent between devices are 32-bit elements; how exact they have to be, the bound alone decides.
No kernel may reach another device: no remote copies, remote signals or barrier semaphores. Data moves between devices by JAX's collectives and lax.ppermute only.
A program may use at most 128 MiB of HBM per device.

v0:
```python
import jax
import jax.numpy as jnp
from jax import lax
from jax.sharding import PartitionSpec as P

STEPS = 4
CAP = 128
COEFFS = (-205.0 / 72.0, 8.0 / 5.0, -1.0 / 5.0, 8.0 / 315.0, -1.0 / 560.0)


def with_halo(block, sides, width):
    for axis, dim in sides:
        count = lax.axis_size(axis)
        forward = [(i, i + 1) for i in range(count - 1)]
        backward = [(target, source) for source, target in forward]
        low = lax.ppermute(
            lax.slice_in_dim(block, block.shape[dim] - width, None, axis=dim), axis, forward
        )
        high = lax.ppermute(lax.slice_in_dim(block, 0, width, axis=dim), axis, backward)
        block = jnp.concatenate([low, block, high], axis=dim)
    return block


def laplace(padded):
    cells_x = padded.shape[0] - 8
    cells_y = padded.shape[1] - 8
    cells_z = padded.shape[2] - 8
    center = padded[4 : 4 + cells_x, 4 : 4 + cells_y, 4 : 4 + cells_z]
    total = 3.0 * COEFFS[0] * center
    for offset in range(1, 5):
        pairs = (
            padded[4 + offset : 4 + offset + cells_x, 4 : 4 + cells_y, 4 : 4 + cells_z]
            + padded[4 - offset : 4 - offset + cells_x, 4 : 4 + cells_y, 4 : 4 + cells_z]
        )
        pairs = (
            pairs
            + padded[4 : 4 + cells_x, 4 + offset : 4 + offset + cells_y, 4 : 4 + cells_z]
            + padded[4 : 4 + cells_x, 4 - offset : 4 - offset + cells_y, 4 : 4 + cells_z]
        )
        pairs = (
            pairs
            + padded[4 : 4 + cells_x, 4 : 4 + cells_y, 4 + offset : 4 + offset + cells_z]
            + padded[4 : 4 + cells_x, 4 : 4 + cells_y, 4 - offset : 4 - offset + cells_z]
        )
        total = total + COEFFS[offset] * pairs
    return total


def accumulate(grad_total, term):
    return grad_total + term


def inject_by_slots(surf_dest, surf_cell, surf_vals, cells):
    owners = lax.axis_size("tgt")
    target = surf_dest[:, 0]
    onehot_table = (target[:, None] == jnp.arange(owners, dtype=jnp.int32)[None, :]).astype(
        jnp.int32
    )
    ranks = jnp.sum((jnp.cumsum(onehot_table, axis=0) - 1) * onehot_table, axis=1)
    position = target * CAP + ranks
    cell_row = (
        jnp.full((owners * CAP,), -1.0, jnp.float32).at[position].set(surf_cell.astype(jnp.float32))
    )
    value_rows = jnp.zeros((STEPS, owners * CAP), jnp.float32).at[:, position].set(surf_vals[0])
    packed = jnp.concatenate([cell_row[None, :], value_rows], axis=0).reshape(
        STEPS + 1, owners, CAP
    )
    arrived = lax.all_to_all(packed, "tgt", split_axis=1, concat_axis=1, tiled=True)
    flat = arrived.reshape(STEPS + 1, owners * CAP)
    where_to = jnp.where(flat[0] >= 0.0, flat[0], float(cells)).astype(jnp.int32)
    return jnp.zeros((STEPS, cells), jnp.float32).at[:, where_to].add(flat[1:], mode="drop")


def on_device(adjoint_now, adjoint_later, courant, fwd_acc, surf_dest, surf_cell, surf_vals):
    current = adjoint_now[0]
    later_field = adjoint_later[0]
    grid_shape = current.shape
    cells = grid_shape[0] * grid_shape[1] * grid_shape[2]
    inject = inject_by_slots(surf_dest, surf_cell, surf_vals, cells)
    grad_total = jnp.zeros(grid_shape, jnp.float32)
    square = courant * courant
    for step in range(STEPS):
        padded = with_halo(current, (("tgt", 0),), 4)
        padded = jnp.pad(padded, ((0, 0), (4, 4), (4, 4)))
        fresh = (
            2.0 * current
            - later_field
            + square * laplace(padded)
            + inject[step].reshape(grid_shape)
        )
        term = fwd_acc[0, step].astype(jnp.float32) * fresh / courant
        grad_total = accumulate(grad_total, term)
        later_field = current
        current = fresh
    grad_total = lax.psum(grad_total, "shot")
    return (current[None], grad_total)


def solution(mesh):
    in_specs = (
        P(("grp", "shot"), "tgt", None, None),
        P(("grp", "shot"), "tgt", None, None),
        P("tgt", None, None),
        P(("grp", "shot"), None, "tgt", None, None),
        P("tgt", None),
        P("tgt"),
        P(("grp", "shot"), None, "tgt"),
    )
    out_specs = (P(("grp", "shot"), "tgt", None, None), P(("grp", "tgt"), None, None))
    return jax.shard_map(
        on_device, mesh=mesh, in_specs=in_specs, out_specs=out_specs, check_vma=False
    )
```

profile of v0, /device:TPU:0, one launch (start us, length us, event | category | flops | bytes accessed | tf_op | source)
XLA Modules:
  0.0 151.7 jit_solution(5388115988067436681)
XLA Ops:
  7.2 0.7 compare_convert_fusion
  7.8 1.2 reduce-window.6
  9.1 0.1 slice.502
  9.1 0.1 copy.22
  9.3 0.1 copy.23
  9.4 0.1 add_bitcast_fusion
  9.4 0.7 fusion.119
  10.1 0.7 compare_select_fusion.2
  10.8 0.8 copy.24
  11.7 1.2 scatter_custom_fusion.1
  12.9 0.1 copy.26
  13.0 0.7 convert_element_type.48
  13.7 1.4 scatter_custom_fusion
  15.1 0.6 pad_maximum_fusion.8
  15.7 6.3 %all-to-all-start = ((f32[5,4,128]{2,0,1:T(8,128)}), f32[5,4,128]{2,0,1:T(8,128)S(1)}, u32[]{:S(2)}, u32[]{:S(2)}) async-start(f32[5,4,128]{2,0,1:T(8,128)} %pad_maximum_fusion.8), calls=%async_computation | async-start | bytes 32768 | tf_op jit(solution)/shard_map/all_to_all | solution.py:68
  22.0 0.0 all-reduce.6.cloned.1.call-start
  22.0 1.3 collective-permute-start
  23.3 4.6 %collective-permute-start.1 = (f32[4,32,256]{2,1,0:T(8,128)}, f32[4,32,256]{2,1,0:T(8,128)S(1)}, u32[]{:S(2)}, u32[]{:S(2)}) collective-permute-start(f32[4,32,256]{2,1,0:T(8,128)} %bitcast.55), channel_id=1, source_target_pairs={{0,4},{4,8},{8,12},{1,5},{5,9},{9,13},{2,6},{6,10},{10,14},{3,7},{... | collective-permute-start | bytes 393224 | tf_op jit(solution)/shard_map/ppermute | solution.py:16
  27.9 0.0 all-to-all-done
  27.9 0.1 copy.27
  28.1 9.0 %scatter_custom_fusion.2 = f32[4,32768]{0,1:T(8,128)} fusion(s32[512]{0:T(512)S(1)} %bitcast.66, f32[512,4]{1,0:T(8,128)S(1)} %copy.27, f32[]{:T(128)} %constant.16.clone.1), kind=kCustom, calls=%fused_computation.7 | custom fusion | flops 2048 | bytes 524292 | tf_op jit(solution)/shard_map/scatter-add | solution.py:71
  37.1 0.0 copy-start.1
  37.1 0.0 copy-start
  37.1 0.0 copy-start.3
  37.1 0.0 copy-start.2
  37.1 41.4 %slice_reduce_fusion.3 = (f32[32768]{0:T(1024)S(1)}, f32[32768]{0:T(1024)S(1)}, f32[32768]{0:T(1024)S(1)}, f32[32768]{0:T(1024)S(1)}) fusion(f32[4,32768]{0,1:T(8,128)} %scatter_custom_fusion.2), kind=kLoop, calls=%fused_computation.6 | loop fusion | bytes 1048576 | tf_op jit(solution)/shard_map/slice | solution.py:89
  78.5 0.0 collective-permute-done
  78.5 0.0 collective-permute-done.1
  78.5 0.0 copy-done.1
  78.5 0.3 select_maximum_fusion.6
  78.8 0.0 copy-done
  78.8 0.0 copy-done.3
  78.8 0.6 fusion.86
  79.4 1.3 collective-permute-start.2
  80.7 4.6 %collective-permute-start.3 = (f32[4,32,256]{2,1,0:T(8,128)S(1)}, f32[4,32,256]{2,1,0:T(8,128)S(1)}, u32[]{:S(2)}, u32[]{:S(2)}) collective-permute-start(f32[4,32,256]{2,1,0:T(8,128)S(1)} %fusion.86), channel_id=1, source_target_pairs={{0,4},{4,8},{8,12},{1,5},{5,9},{9,13},{2,6},{6,10},{10,14},{3,7},{... | collective-permute-start | bytes 393224 | tf_op jit(solution)/shard_map/ppermute | solution.py:16
  85.3 1.0 collective-permute-done.2
  86.3 1.5 collective-permute-done.3
  87.8 0.3 select_maximum_fusion.4
  88.0 0.6 fusion.63
  88.6 1.3 collective-permute-start.4
  89.9 5.0 %collective-permute-start.5 = (f32[4,32,256]{2,1,0:T(8,128)S(1)}, f32[4,32,256]{2,1,0:T(8,128)S(1)}, u32[]{:S(2)}, u32[]{:S(2)}) collective-permute-start(f32[4,32,256]{2,1,0:T(8,128)S(1)} %fusion.63), channel_id=1, source_target_pairs={{0,4},{4,8},{8,12},{1,5},{5,9},{9,13},{2,6},{6,10},{10,14},{3,7},{... | collective-permute-start | bytes 393224 | tf_op jit(solution)/shard_map/ppermute | solution.py:16
  95.0 1.0 collective-permute-done.4
  95.9 1.5 collective-permute-done.5
  97.4 0.3 select_maximum_fusion.2
  97.7 0.6 fusion.40
  98.3 1.3 collective-permute-start.6
  99.6 5.0 %collective-permute-start.7 = (f32[4,32,256]{2,1,0:T(8,128)S(1)}, f32[4,32,256]{2,1,0:T(8,128)S(1)}, u32[]{:S(2)}, u32[]{:S(2)}) collective-permute-start(f32[4,32,256]{2,1,0:T(8,128)S(1)} %fusion.40), channel_id=1, source_target_pairs={{0,4},{4,8},{8,12},{1,5},{5,9},{9,13},{2,6},{6,10},{10,14},{3,7},{... | collective-permute-start | bytes 393224 | tf_op jit(solution)/shard_map/ppermute | solution.py:16
  104.6 1.0 collective-permute-done.6
  105.6 1.5 collective-permute-done.7
  107.1 0.3 select_maximum_fusion
  107.4 0.0 copy-done.2
  107.4 1.3 fusion.110
  108.7 0.0 all-reduce.6.cloned.1.call-update
  108.7 34.6 %all-reduce.6.cloned.1.call-done = f32[4,32,256]{2,1,0:T(8,128)} async-done(((f32[4,32,256]{2,1,0:T(8,128)}), f32[4,32,256]{2,1,0:T(8,128)}) %all-reduce.6.cloned.1.call-update) | async-done | bytes 131088 | tf_op jit(solution)/shard_map/psum | solution.py:95
  143.3 1.6 %copy.31 = f32[4,32,256]{2,1,0:T(8,128)} copy(f32[4,32,256]{2,1,0:T(8,128)} %all-reduce.6.cloned.1.call-done) | data formatting | bytes 262144
  (8 shorter events, 0.2 us)
Async XLA Ops:
  15.7 12.2 %all-to-all-start = ((f32[5,4,128]{2,0,1:T(8,128)}), f32[5,4,128]{2,0,1:T(8,128)S(1)}, u32[]{:S(2)}, u32[]{:S(2)}) async-start(f32[5,4,128]{2,0,1:T(8,128)} %pad_maximum_fusion.8), calls=%async_computation | async-start | bytes 32768 | tf_op jit(solution)/shard_map/all_to_all | solution.py:68
  22.0 121.2 %all-reduce.6.cloned.1.call-start = ((), (), s32[]{:S(2)}) async-start(), calls=%async_computation.1 | async-start | bytes 262144 | tf_op jit(solution)/shard_map/psum | solution.py:95
  22.0 56.5 %collective-permute-start = (f32[4,32,256]{2,1,0:T(8,128)}, f32[4,32,256]{2,1,0:T(8,128)S(1)}, u32[]{:S(2)}, u32[]{:S(2)}) collective-permute-start(f32[4,32,256]{2,1,0:T(8,128)} %bitcast.54), channel_id=1, source_target_pairs={{4,0},{8,4},{12,8},{5,1},{9,5},{13,9},{6,2},{10,6},{14,10},{7,3},{... | collective-permute-start | bytes 393224 | tf_op jit(solution)/shard_map/ppermute | solution.py:19
  23.3 55.2 %collective-permute-start.1 = (f32[4,32,256]{2,1,0:T(8,128)}, f32[4,32,256]{2,1,0:T(8,128)S(1)}, u32[]{:S(2)}, u32[]{:S(2)}) collective-permute-start(f32[4,32,256]{2,1,0:T(8,128)} %bitcast.55), channel_id=1, source_target_pairs={{0,4},{4,8},{8,12},{1,5},{5,9},{9,13},{2,6},{6,10},{10,14},{3,7},{... | collective-permute-start | bytes 393224 | tf_op jit(solution)/shard_map/ppermute | solution.py:16
  37.1 41.5 %copy-start.1 = (f32[1,4,32,256]{3,2,1,0:T(8,128)S(1)}, f32[1,4,32,256]{3,2,1,0:T(8,128)}, u32[]{:S(2)}) copy-start(f32[1,4,32,256]{3,2,1,0:T(8,128)} %param.7) | copy-start | bytes 393220
  37.1 41.7 %copy-start = (f32[4,32,256]{2,1,0:T(8,128)S(1)}, f32[4,32,256]{2,1,0:T(8,128)}, u32[]{:S(2)}) copy-start(f32[4,32,256]{2,1,0:T(8,128)} %param.9) | copy-start | bytes 393220
  37.1 41.7 %copy-start.3 = (f32[1,4,32,256]{3,2,1,0:T(8,128)S(1)}, f32[1,4,32,256]{3,2,1,0:T(8,128)}, u32[]{:S(2)}) copy-start(f32[1,4,32,256]{3,2,1,0:T(8,128)} %param.8) | copy-start | bytes 393220
  37.1 70.3 %copy-start.2 = (bf16[1,4,4,32,256]{4,3,2,1,0:T(8,128)(2,1)S(1)}, bf16[1,4,4,32,256]{4,3,2,1,0:T(8,128)(2,1)}, u32[]{:S(2)}) copy-start(bf16[1,4,4,32,256]{4,3,2,1,0:T(8,128)(2,1)} %param.10) | copy-start | bytes 786436
  79.4 6.9 %collective-permute-start.2 = (f32[4,32,256]{2,1,0:T(8,128)S(1)}, f32[4,32,256]{2,1,0:T(8,128)S(1)}, u32[]{:S(2)}, u32[]{:S(2)}) collective-permute-start(f32[4,32,256]{2,1,0:T(8,128)S(1)} %fusion.86), channel_id=1, source_target_pairs={{4,0},{8,4},{12,8},{5,1},{9,5},{13,9},{6,2},{10,6},{14,10},{7,3},{... | collective-permute-start | bytes 393224 | tf_op jit(solution)/shard_map/ppermute | solution.py:19
  80.7 7.1 %collective-permute-start.3 = (f32[4,32,256]{2,1,0:T(8,128)S(1)}, f32[4,32,256]{2,1,0:T(8,128)S(1)}, u32[]{:S(2)}, u32[]{:S(2)}) collective-permute-start(f32[4,32,256]{2,1,0:T(8,128)S(1)} %fusion.86), channel_id=1, source_target_pairs={{0,4},{4,8},{8,12},{1,5},{5,9},{9,13},{2,6},{6,10},{10,14},{3,7},{... | collective-permute-start | bytes 393224 | tf_op jit(solution)/shard_map/ppermute | solution.py:16
  88.6 7.3 %collective-permute-start.4 = (f32[4,32,256]{2,1,0:T(8,128)S(1)}, f32[4,32,256]{2,1,0:T(8,128)S(1)}, u32[]{:S(2)}, u32[]{:S(2)}) collective-permute-start(f32[4,32,256]{2,1,0:T(8,128)S(1)} %fusion.63), channel_id=1, source_target_pairs={{4,0},{8,4},{12,8},{5,1},{9,5},{13,9},{6,2},{10,6},{14,10},{7,3},{... | collective-permute-start | bytes 393224 | tf_op jit(solution)/shard_map/ppermute | solution.py:19
  89.9 7.5 %collective-permute-start.5 = (f32[4,32,256]{2,1,0:T(8,128)S(1)}, f32[4,32,256]{2,1,0:T(8,128)S(1)}, u32[]{:S(2)}, u32[]{:S(2)}) collective-permute-start(f32[4,32,256]{2,1,0:T(8,128)S(1)} %fusion.63), channel_id=1, source_target_pairs={{0,4},{4,8},{8,12},{1,5},{5,9},{9,13},{2,6},{6,10},{10,14},{3,7},{... | collective-permute-start | bytes 393224 | tf_op jit(solution)/shard_map/ppermute | solution.py:16
  98.3 7.3 %collective-permute-start.6 = (f32[4,32,256]{2,1,0:T(8,128)S(1)}, f32[4,32,256]{2,1,0:T(8,128)S(1)}, u32[]{:S(2)}, u32[]{:S(2)}) collective-permute-start(f32[4,32,256]{2,1,0:T(8,128)S(1)} %fusion.40), channel_id=1, source_target_pairs={{4,0},{8,4},{12,8},{5,1},{9,5},{13,9},{6,2},{10,6},{14,10},{7,3},{... | collective-permute-start | bytes 393224 | tf_op jit(solution)/shard_map/ppermute | solution.py:19
  99.6 7.5 %collective-permute-start.7 = (f32[4,32,256]{2,1,0:T(8,128)S(1)}, f32[4,32,256]{2,1,0:T(8,128)S(1)}, u32[]{:S(2)}, u32[]{:S(2)}) collective-permute-start(f32[4,32,256]{2,1,0:T(8,128)S(1)} %fusion.40), channel_id=1, source_target_pairs={{0,4},{4,8},{8,12},{1,5},{5,9},{9,13},{2,6},{6,10},{10,14},{3,7},{... | collective-permute-start | bytes 393224 | tf_op jit(solution)/shard_map/ppermute | solution.py:16
Sparse Core Ops, SparseCore 0:
  108.8 34.3 all-reduce.5
where the time goes:
time: 152 us
  local copies, waits for them, and re-layouts  47.1 us (31%)
  waiting for transfers between devices  41.9 us (28%)
  starting transfers between devices  30.6 us (20%)
  other arithmetic  17.8 us (12%)
  between operations  14.3 us (9%)
    slice x1, local copies, waits for them, and re-layouts, on_device(): inject[step].reshape(grid_shape)  41.4 us
    psum x1, waiting for transfers between devices, on_device(): grad_total = lax.psum(grad_total, 'shot')  34.6 us
    ppermute x4, starting transfers between devices, with_halo(): lax.ppermute(lax.slice_in_dim(block, block.shape[dim] - width, None, axis...  19.1 us
    scatter-add x1, other arithmetic, inject_by_slots(): jnp.zeros((STEPS, cells), jnp.float32).at[:, where_to]  8.99 us
    all_to_all x1, starting transfers between devices, inject_by_slots(): lax.all_to_all(packed, 'tgt', split_axis=1, concat_axis=1, tiled=True)  6.32 us
    ppermute x4, starting transfers between devices, with_halo(): lax.ppermute(lax.slice_in_dim(block, 0, width, axis=dim), axis, backward)  5.16 us
    ppermute x4, waiting for transfers between devices, with_halo(): lax.ppermute(lax.slice_in_dim(block, block.shape[dim] - width, None, axis...  4.49 us
  transfers between devices with their start and end apart: 10, of which 7 were waited for; matrix products, arithmetic and copies ran while one was open for 33% of the time, Pallas kernels for 0%

commit v1 on v0

--- a/solution.py
+++ b/solution.py
@@ -6,6 +6,12 @@
 STEPS = 4
 CAP = 128
 COEFFS = (-205.0 / 72.0, 8.0 / 5.0, -1.0 / 5.0, 8.0 / 315.0, -1.0 / 560.0)
+
+
+def stacked_exchange(block, axis, split, join):
+    parts = jnp.split(block, lax.axis_size(axis), axis=split)
+    got = lax.all_to_all(jnp.stack(parts), axis, 0, 0)
+    return jnp.concatenate(got, axis=join)
 
 
 def with_halo(block, sides, width):
@@ -65,7 +71,7 @@
     packed = jnp.concatenate([cell_row[None, :], value_rows], axis=0).reshape(
         STEPS + 1, owners, CAP
     )
-    arrived = lax.all_to_all(packed, "tgt", split_axis=1, concat_axis=1, tiled=True)
+    arrived = stacked_exchange(packed, "tgt", 1, 1)
     flat = arrived.reshape(STEPS + 1, owners * CAP)
     where_to = jnp.where(flat[0] >= 0.0, flat[0], float(cells)).astype(jnp.int32)
     return jnp.zeros((STEPS, cells), jnp.float32).at[:, where_to].add(flat[1:], mode="drop")

time: 152 us -> 152 us (level)
  no operation moved by 1% of the time
where the time goes in v1:
time: 152 us
  local copies, waits for them, and re-layouts  47.1 us (31%)
  waiting for transfers between devices  41.9 us (28%)
  starting transfers between devices  30.6 us (20%)
  other arithmetic  17.8 us (12%)
  between operations  14.3 us (9%)
    slice x1, local copies, waits for them, and re-layouts, on_device(): inject[step].reshape(grid_shape)  41.4 us
    psum x1, waiting for transfers between devices, on_device(): grad_total = lax.psum(grad_total, 'shot')  34.6 us
    ppermute x4, starting transfers between devices, with_halo(): lax.ppermute(lax.slice_in_dim(block, block.shape[dim] - width, None, axis...  19.1 us
    scatter-add x1, other arithmetic, inject_by_slots(): jnp.zeros((STEPS, cells), jnp.float32).at[:, where_to]  8.99 us
    all_to_all x1, starting transfers between devices, stacked_exchange(): got = lax.all_to_all(jnp.stack(parts), axis, 0, 0)  6.32 us
    ppermute x4, starting transfers between devices, with_halo(): lax.ppermute(lax.slice_in_dim(block, 0, width, axis=dim), axis, backward)  5.16 us
    ppermute x4, waiting for transfers between devices, with_halo(): lax.ppermute(lax.slice_in_dim(block, block.shape[dim] - width, None, axis...  4.49 us
  transfers between devices with their start and end apart: 10, of which 7 were waited for; matrix products, arithmetic and copies ran while one was open for 33% of the time, Pallas kernels for 0%

profile of v1, /device:TPU:0, one launch (start us, length us, event | category | flops | bytes accessed | tf_op | source)
XLA Modules:
  0.0 151.7 jit_solution(13786091490973836141)
XLA Ops:
  7.2 0.7 compare_convert_fusion
  7.8 1.2 reduce-window.6
  9.1 0.1 slice.502
  9.1 0.1 copy.24
  9.3 0.1 copy.25
  9.4 0.1 add_bitcast_fusion
  9.4 0.7 fusion.119
  10.1 0.7 compare_select_fusion.2
  10.8 0.8 copy.26
  11.7 1.2 scatter_custom_fusion.1
  12.9 0.1 copy.27
  13.0 0.7 convert_element_type.48
  13.7 1.4 scatter_custom_fusion
  15.1 0.6 pad_maximum_fusion.8
  15.7 6.3 %all-to-all-start = ((f32[4,5,1,128]{3,2,1,0:T(1,128)}), f32[4,5,1,128]{3,2,1,0:T(1,128)S(1)}, u32[]{:S(2)}, u32[]{:S(2)}) async-start(f32[4,5,1,128]{3,2,1,0:T(1,128)} %pad_maximum_fusion.8), calls=%async_computation | async-start | bytes 20480 | tf_op jit(solution)/shard_map/all_to_all | solution.py:13
  22.0 0.0 all-reduce.6.cloned.1.call-start
  22.0 1.3 collective-permute-start
  23.3 4.6 %collective-permute-start.1 = (f32[4,32,256]{2,1,0:T(8,128)}, f32[4,32,256]{2,1,0:T(8,128)S(1)}, u32[]{:S(2)}, u32[]{:S(2)}) collective-permute-start(f32[4,32,256]{2,1,0:T(8,128)} %bitcast.61), channel_id=1, source_target_pairs={{0,4},{4,8},{8,12},{1,5},{5,9},{9,13},{2,6},{6,10},{10,14},{3,7},{... | collective-permute-start | bytes 393224 | tf_op jit(solution)/shard_map/ppermute | solution.py:22
  27.9 0.0 all-to-all-done
  27.9 0.1 copy.29
  28.1 9.0 %scatter_custom_fusion.2 = f32[4,32768]{0,1:T(8,128)} fusion(s32[512]{0:T(512)S(1)} %bitcast.75, f32[512,4]{1,0:T(8,128)S(1)} %copy.29, f32[]{:T(128)} %constant.16.clone.1), kind=kCustom, calls=%fused_computation.7 | custom fusion | flops 2048 | bytes 524292 | tf_op jit(solution)/shard_map/scatter-add | solution.py:77
  37.1 0.0 copy-start.1
  37.1 0.0 copy-start
  37.1 0.0 copy-start.3
  37.1 0.0 copy-start.2
  37.1 41.4 %slice_reduce_fusion.3 = (f32[32768]{0:T(1024)S(1)}, f32[32768]{0:T(1024)S(1)}, f32[32768]{0:T(1024)S(1)}, f32[32768]{0:T(1024)S(1)}) fusion(f32[4,32768]{0,1:T(8,128)} %scatter_custom_fusion.2), kind=kLoop, calls=%fused_computation.6 | loop fusion | bytes 1048576 | tf_op jit(solution)/shard_map/slice | solution.py:95
  78.5 0.0 collective-permute-done
  78.5 0.0 collective-permute-done.1
  78.5 0.0 copy-done.1
  78.5 0.3 select_maximum_fusion.6
  78.8 0.0 copy-done
  78.8 0.0 copy-done.3
  78.8 0.6 fusion.86
  79.4 1.3 collective-permute-start.2
  80.7 4.6 %collective-permute-start.3 = (f32[4,32,256]{2,1,0:T(8,128)S(1)}, f32[4,32,256]{2,1,0:T(8,128)S(1)}, u32[]{:S(2)}, u32[]{:S(2)}) collective-permute-start(f32[4,32,256]{2,1,0:T(8,128)S(1)} %fusion.86), channel_id=1, source_target_pairs={{0,4},{4,8},{8,12},{1,5},{5,9},{9,13},{2,6},{6,10},{10,14},{3,7},{... | collective-permute-start | bytes 393224 | tf_op jit(solution)/shard_map/ppermute | solution.py:22
  85.3 1.0 collective-permute-done.2
  86.3 1.5 collective-permute-done.3
  87.8 0.3 select_maximum_fusion.4
  88.1 0.6 fusion.63
  88.7 1.3 collective-permute-start.4
  90.0 5.0 %collective-permute-start.5 = (f32[4,32,256]{2,1,0:T(8,128)S(1)}, f32[4,32,256]{2,1,0:T(8,128)S(1)}, u32[]{:S(2)}, u32[]{:S(2)}) collective-permute-start(f32[4,32,256]{2,1,0:T(8,128)S(1)} %fusion.63), channel_id=1, source_target_pairs={{0,4},{4,8},{8,12},{1,5},{5,9},{9,13},{2,6},{6,10},{10,14},{3,7},{... | collective-permute-start | bytes 393224 | tf_op jit(solution)/shard_map/ppermute | solution.py:22
  95.0 1.0 collective-permute-done.4
  96.0 1.5 collective-permute-done.5
  97.5 0.3 select_maximum_fusion.2
  97.7 0.6 fusion.40
  98.3 1.3 collective-permute-start.6
  99.6 5.0 %collective-permute-start.7 = (f32[4,32,256]{2,1,0:T(8,128)S(1)}, f32[4,32,256]{2,1,0:T(8,128)S(1)}, u32[]{:S(2)}, u32[]{:S(2)}) collective-permute-start(f32[4,32,256]{2,1,0:T(8,128)S(1)} %fusion.40), channel_id=1, source_target_pairs={{0,4},{4,8},{8,12},{1,5},{5,9},{9,13},{2,6},{6,10},{10,14},{3,7},{... | collective-permute-start | bytes 393224 | tf_op jit(solution)/shard_map/ppermute | solution.py:22
  104.7 1.0 collective-permute-done.6
  105.6 1.5 collective-permute-done.7
  107.1 0.3 select_maximum_fusion
  107.4 0.0 copy-done.2
  107.4 1.3 fusion.110
  108.7 0.0 all-reduce.6.cloned.1.call-update
  108.7 34.6 %all-reduce.6.cloned.1.call-done = f32[4,32,256]{2,1,0:T(8,128)} async-done(((f32[4,32,256]{2,1,0:T(8,128)}), f32[4,32,256]{2,1,0:T(8,128)}) %all-reduce.6.cloned.1.call-update) | async-done | bytes 131088 | tf_op jit(solution)/shard_map/psum | solution.py:101
  143.3 1.6 %copy.33 = f32[4,32,256]{2,1,0:T(8,128)} copy(f32[4,32,256]{2,1,0:T(8,128)} %all-reduce.6.cloned.1.call-done) | data formatting | bytes 262144
  (9 shorter events, 0.2 us)
Async XLA Ops:
  15.7 12.2 %all-to-all-start = ((f32[4,5,1,128]{3,2,1,0:T(1,128)}), f32[4,5,1,128]{3,2,1,0:T(1,128)S(1)}, u32[]{:S(2)}, u32[]{:S(2)}) async-start(f32[4,5,1,128]{3,2,1,0:T(1,128)} %pad_maximum_fusion.8), calls=%async_computation | async-start | bytes 20480 | tf_op jit(solution)/shard_map/all_to_all | solution.py:13
  22.0 121.2 %all-reduce.6.cloned.1.call-start = ((), (), s32[]{:S(2)}) async-start(), calls=%async_computation.1 | async-start | bytes 262144 | tf_op jit(solution)/shard_map/psum | solution.py:101
  22.0 56.5 %collective-permute-start = (f32[4,32,256]{2,1,0:T(8,128)}, f32[4,32,256]{2,1,0:T(8,128)S(1)}, u32[]{:S(2)}, u32[]{:S(2)}) collective-permute-start(f32[4,32,256]{2,1,0:T(8,128)} %bitcast.60), channel_id=1, source_target_pairs={{4,0},{8,4},{12,8},{5,1},{9,5},{13,9},{6,2},{10,6},{14,10},{7,3},{... | collective-permute-start | bytes 393224 | tf_op jit(solution)/shard_map/ppermute | solution.py:25
  23.3 55.2 %collective-permute-start.1 = (f32[4,32,256]{2,1,0:T(8,128)}, f32[4,32,256]{2,1,0:T(8,128)S(1)}, u32[]{:S(2)}, u32[]{:S(2)}) collective-permute-start(f32[4,32,256]{2,1,0:T(8,128)} %bitcast.61), channel_id=1, source_target_pairs={{0,4},{4,8},{8,12},{1,5},{5,9},{9,13},{2,6},{6,10},{10,14},{3,7},{... | collective-permute-start | bytes 393224 | tf_op jit(solution)/shard_map/ppermute | solution.py:22
  37.1 41.5 %copy-start.1 = (f32[1,4,32,256]{3,2,1,0:T(8,128)S(1)}, f32[1,4,32,256]{3,2,1,0:T(8,128)}, u32[]{:S(2)}) copy-start(f32[1,4,32,256]{3,2,1,0:T(8,128)} %param.7) | copy-start | bytes 393220
  37.1 41.7 %copy-start = (f32[4,32,256]{2,1,0:T(8,128)S(1)}, f32[4,32,256]{2,1,0:T(8,128)}, u32[]{:S(2)}) copy-start(f32[4,32,256]{2,1,0:T(8,128)} %param.9) | copy-start | bytes 393220
  37.1 41.7 %copy-start.3 = (f32[1,4,32,256]{3,2,1,0:T(8,128)S(1)}, f32[1,4,32,256]{3,2,1,0:T(8,128)}, u32[]{:S(2)}) copy-start(f32[1,4,32,256]{3,2,1,0:T(8,128)} %param.8) | copy-start | bytes 393220
  37.1 70.3 %copy-start.2 = (bf16[1,4,4,32,256]{4,3,2,1,0:T(8,128)(2,1)S(1)}, bf16[1,4,4,32,256]{4,3,2,1,0:T(8,128)(2,1)}, u32[]{:S(2)}) copy-start(bf16[1,4,4,32,256]{4,3,2,1,0:T(8,128)(2,1)} %param.10) | copy-start | bytes 786436
  79.4 6.9 %collective-permute-start.2 = (f32[4,32,256]{2,1,0:T(8,128)S(1)}, f32[4,32,256]{2,1,0:T(8,128)S(1)}, u32[]{:S(2)}, u32[]{:S(2)}) collective-permute-start(f32[4,32,256]{2,1,0:T(8,128)S(1)} %fusion.86), channel_id=1, source_target_pairs={{4,0},{8,4},{12,8},{5,1},{9,5},{13,9},{6,2},{10,6},{14,10},{7,3},{... | collective-permute-start | bytes 393224 | tf_op jit(solution)/shard_map/ppermute | solution.py:25
  80.7 7.1 %collective-permute-start.3 = (f32[4,32,256]{2,1,0:T(8,128)S(1)}, f32[4,32,256]{2,1,0:T(8,128)S(1)}, u32[]{:S(2)}, u32[]{:S(2)}) collective-permute-start(f32[4,32,256]{2,1,0:T(8,128)S(1)} %fusion.86), channel_id=1, source_target_pairs={{0,4},{4,8},{8,12},{1,5},{5,9},{9,13},{2,6},{6,10},{10,14},{3,7},{... | collective-permute-start | bytes 393224 | tf_op jit(solution)/shard_map/ppermute | solution.py:22
  88.7 7.3 %collective-permute-start.4 = (f32[4,32,256]{2,1,0:T(8,128)S(1)}, f32[4,32,256]{2,1,0:T(8,128)S(1)}, u32[]{:S(2)}, u32[]{:S(2)}) collective-permute-start(f32[4,32,256]{2,1,0:T(8,128)S(1)} %fusion.63), channel_id=1, source_target_pairs={{4,0},{8,4},{12,8},{5,1},{9,5},{13,9},{6,2},{10,6},{14,10},{7,3},{... | collective-permute-start | bytes 393224 | tf_op jit(solution)/shard_map/ppermute | solution.py:25
  90.0 7.5 %collective-permute-start.5 = (f32[4,32,256]{2,1,0:T(8,128)S(1)}, f32[4,32,256]{2,1,0:T(8,128)S(1)}, u32[]{:S(2)}, u32[]{:S(2)}) collective-permute-start(f32[4,32,256]{2,1,0:T(8,128)S(1)} %fusion.63), channel_id=1, source_target_pairs={{0,4},{4,8},{8,12},{1,5},{5,9},{9,13},{2,6},{6,10},{10,14},{3,7},{... | collective-permute-start | bytes 393224 | tf_op jit(solution)/shard_map/ppermute | solution.py:22
  98.3 7.3 %collective-permute-start.6 = (f32[4,32,256]{2,1,0:T(8,128)S(1)}, f32[4,32,256]{2,1,0:T(8,128)S(1)}, u32[]{:S(2)}, u32[]{:S(2)}) collective-permute-start(f32[4,32,256]{2,1,0:T(8,128)S(1)} %fusion.40), channel_id=1, source_target_pairs={{4,0},{8,4},{12,8},{5,1},{9,5},{13,9},{6,2},{10,6},{14,10},{7,3},{... | collective-permute-start | bytes 393224 | tf_op jit(solution)/shard_map/ppermute | solution.py:25
  99.6 7.5 %collective-permute-start.7 = (f32[4,32,256]{2,1,0:T(8,128)S(1)}, f32[4,32,256]{2,1,0:T(8,128)S(1)}, u32[]{:S(2)}, u32[]{:S(2)}) collective-permute-start(f32[4,32,256]{2,1,0:T(8,128)S(1)} %fusion.40), channel_id=1, source_target_pairs={{0,4},{4,8},{8,12},{1,5},{5,9},{9,13},{2,6},{6,10},{10,14},{3,7},{... | collective-permute-start | bytes 393224 | tf_op jit(solution)/shard_map/ppermute | solution.py:22
Sparse Core Ops, SparseCore 0:
  108.8 34.3 all-reduce.5
